TPU v7x, 256 devices: a whole 4x4x8 slice. The times are simulated.
256 devices in a mesh: group: 8 (over z_hi, core), tensor: 8 (over y, z_lo), seq: 4 (over x).
Axes of the slice: x: 4, y: 4, z: 8 (z_hi: 4, z_lo: 2; z = z_hi * 2 + z_lo), core: 2. Of those that a mesh axis runs over, the one named last changes fastest.
Arguments:
- patches: bfloat16 [8192, 1280], P(('group', 'tensor', 'seq')), may hold values from -6 to 6
- enc_gain: float32 [1280], replicated, may hold values from 0.1 to 1.9
- enc_qkv: bfloat16 [3, 1280, 1280], P(None, None, 'tensor')
- enc_out: bfloat16 [1280, 1280], P('tensor'), may hold values from -0.15625 to 0.15625
- cross_kv: bfloat16 [1280, 2048], P(None, 'tensor'), may hold values from -0.15625 to 0.15625
- key_gain: float32 [128], replicated, may hold values from 0.1 to 1.9
- dec_hidden: bfloat16 [4096, 8192], P(('group', 'seq')), may hold values from -6 to 6
- dec_gain: float32 [8192], replicated, may hold values from 0.1 to 1.9
- query_weight: bfloat16 [8192, 4096], P(None, 'tensor'), may hold values from -0.0625 to 0.0625
- query_gain: float32 [128], replicated, may hold values from 1.5 to 3
- image_of_row: int32 [4096], P(('group', 'seq')), may hold values from 0 to 3
- valid_count: int32 [4096], P(('group', 'seq')), may hold values from 1 to 2048, as said below
Outputs:
- decoded: bfloat16 [4096, 4096], P(('group', 'seq'), 'tensor')
Inputs may be any that keep to these rules, and one draw needn't show every extreme that they name: `valid_count`: every draw has a row reading a whole image and a row reading one patch.
All inputs are finite; a program needn't handle non-finite values.
Results may differ from a plain program's by a relative error of at most 0.028.
The roundings to bfloat16 on the way count: a program that leaves them out, or rounds other values in their place, can miss the bound.
Values may be sent and summed in bfloat16 or wider, within the bound.
No kernel may reach another device: no remote copies, remote signals or barrier semaphores. Data moves between devices by JAX's collectives and lax.ppermute only.
A program may use at most 128 MiB of HBM per device.

v0:
```python
import math
import jax
import jax.numpy as jnp
from jax import lax
from jax.sharding import PartitionSpec as P

EHD = 80
HD = 128
IMAGES = 4
EPSILON = 1e-05


def layer_norm(values, gain_vector):
    mean_value = jnp.mean(values, axis=-1, keepdims=True)
    centered = values - mean_value
    variance = jnp.mean(centered * centered, axis=-1, keepdims=True)
    return centered * lax.rsqrt(variance + EPSILON) * gain_vector


def rms_norm(values, gain_vector):
    square_mean = jnp.mean(values * values, axis=-1, keepdims=True)
    return values * lax.rsqrt(square_mean + EPSILON) * gain_vector


def on_device(
    patches,
    enc_gain,
    enc_qkv,
    enc_out,
    cross_kv,
    key_gain,
    dec_hidden,
    dec_gain,
    query_weight,
    query_gain,
    image_of_row,
    valid_count,
):
    tensor_count = lax.axis_size("tensor")
    seq_count = lax.axis_size("seq")
    patch_rows = patches.shape[0]
    deal_block = patch_rows * seq_count
    gathered = lax.all_gather(patches, "tensor", axis=0, tiled=True)
    row_count = gathered.shape[0]
    normed = layer_norm(gathered.astype(jnp.float32), enc_gain).astype(jnp.bfloat16)
    local_width = enc_qkv.shape[2]
    local_heads = local_width // EHD
    query_part = (
        jnp.dot(normed, enc_qkv[0], preferred_element_type=jnp.float32)
        .astype(jnp.bfloat16)
        .reshape(row_count, local_heads, EHD)
    )
    key_part = jnp.dot(normed, enc_qkv[1], preferred_element_type=jnp.float32).astype(jnp.bfloat16)
    value_part = jnp.dot(normed, enc_qkv[2], preferred_element_type=jnp.float32).astype(
        jnp.bfloat16
    )

    def patch_number(gathered_index):
        shard_number = gathered_index // row_count
        within = gathered_index % row_count
        source_tensor = within // patch_rows
        source_row = within % patch_rows
        source_group = shard_number // seq_count
        source_seq = shard_number % seq_count
        return (
            (source_group * tensor_count + source_tensor) * seq_count + source_seq
        ) * patch_rows + source_row

    def image_number(patch_index):
        return patch_index // deal_block % IMAGES

    own_index = jnp.arange(row_count, dtype=jnp.int32)
    own_shard = lax.axis_index("group") * seq_count + lax.axis_index("seq")
    query_image = image_number(patch_number(own_shard * row_count + own_index))
    running_max = jnp.full((local_heads, row_count), -1e30, jnp.float32)
    key_shard = lax.all_gather(key_part, ("group", "seq"), axis=0, tiled=True)
    value_shard = lax.all_gather(value_part, ("group", "seq"), axis=0, tiled=True)
    piece_rows = key_shard.shape[0]
    key_index = jnp.arange(piece_rows, dtype=jnp.int32)
    key_image = image_number(patch_number(key_index))
    same_image = (query_image[:, None] == key_image[None, :])[None]
    key_heads = key_shard.reshape(piece_rows, local_heads, EHD)
    value_heads = value_shard.reshape(piece_rows, local_heads, EHD)
    scores = jnp.einsum(
        "rhd,khd->hrk", query_part, key_heads, preferred_element_type=jnp.float32
    ) / math.sqrt(EHD)
    masked = jnp.where(same_image, scores, jnp.full_like(scores, -1e30))
    new_max = jnp.maximum(running_max, jnp.max(masked, axis=-1))
    weights = jnp.where(same_image, jnp.exp(scores - new_max[..., None]), jnp.zeros_like(scores))
    new_sum = jnp.sum(weights, axis=-1)
    new_mix = jnp.einsum(
        "hrk,khd->hrd",
        weights.astype(jnp.bfloat16),
        value_heads,
        preferred_element_type=jnp.float32,
    )
    folded = (new_max, new_sum, new_mix)
    final_max, final_sum, final_mix = folded
    attended = (final_mix / final_sum[..., None]).astype(jnp.bfloat16)
    attended = attended.transpose(1, 0, 2).reshape(row_count, local_width)
    total_out = lax.psum(
        jnp.dot(attended, enc_out, preferred_element_type=jnp.float32).astype(jnp.bfloat16),
        "tensor",
    ).astype(jnp.float32)
    encoded = (gathered.astype(jnp.float32) + total_out).astype(jnp.bfloat16)
    kv_local = cross_kv.shape[1] // (2 * HD)
    cross_proj = jnp.dot(encoded, cross_kv, preferred_element_type=jnp.float32).reshape(
        row_count, kv_local, 2, HD
    )
    cross_keys = rms_norm(cross_proj[:, :, 0], key_gain)
    kv_slab = (
        jnp.stack([cross_keys, cross_proj[:, :, 1]], axis=2)
        .astype(jnp.bfloat16)
        .reshape(row_count, kv_local * 2 * HD)
    )
    every_slab = lax.all_gather(kv_slab, ("group", "seq"), axis=0, tiled=True)
    dec_rows = dec_hidden.shape[0]
    dec_normed = rms_norm(dec_hidden.astype(jnp.float32), dec_gain).astype(jnp.bfloat16)
    query_local = query_weight.shape[1] // HD
    group_size = query_local // kv_local
    queries = jnp.dot(dec_normed, query_weight, preferred_element_type=jnp.float32).reshape(
        dec_rows, query_local, HD
    )
    queries = (rms_norm(queries, query_gain) / math.sqrt(HD)).astype(jnp.bfloat16)
    queries = queries.reshape(dec_rows, kv_local, group_size, HD)
    slab_rows = every_slab.shape[0]
    slab_view = every_slab.reshape(slab_rows, kv_local, 2, HD)
    patch_index = patch_number(jnp.arange(slab_rows, dtype=jnp.int32))
    slab_image = image_number(patch_index)
    slab_position = patch_index // (deal_block * IMAGES) * deal_block + patch_index % deal_block
    allowed = (slab_image[None, :] == image_of_row[:, None]) & (
        slab_position[None, :] < valid_count[:, None]
    )
    scores = jnp.einsum(
        "rgqd,kgd->gqrk", queries, slab_view[:, :, 0], preferred_element_type=jnp.float32
    )
    weights = jnp.where(allowed[None, None], jnp.exp(scores), jnp.zeros_like(scores))
    weight_sum = jnp.sum(weights, axis=-1)
    mixture = jnp.einsum(
        "gqrk,kgd->rgqd",
        weights.astype(jnp.bfloat16),
        slab_view[:, :, 1],
        preferred_element_type=jnp.float32,
    )
    result = mixture / weight_sum.transpose(2, 0, 1)[..., None]
    return result.astype(jnp.bfloat16).reshape(dec_rows, query_local * HD)


def solution(mesh):
    in_specs = (
        P(("group", "tensor", "seq"), None),
        P(),
        P(None, None, "tensor"),
        P("tensor", None),
        P(None, "tensor"),
        P(),
        P(("group", "seq"), None),
        P(),
        P(None, "tensor"),
        P(),
        P(("group", "seq")),
        P(("group", "seq")),
    )
    out_specs = P(("group", "seq"), "tensor")
    return jax.shard_map(
        on_device, mesh=mesh, in_specs=in_specs, out_specs=out_specs, check_vma=False
    )
```

profile of v0, /device:TPU:1, one launch (start us, length us, event | category | flops | bytes accessed | tf_op | source)
XLA Modules:
  0.0 340.4 jit_solution(16745044006763906302)
XLA Ops:
  6.5 26.6 %all_gather.12 = bf16[256,1280]{1,0:T(8,128)(2,1)S(1)} all-gather(bf16[32,1280]{1,0:T(8,128)(2,1)} %param.12), channel_id=1, replica_groups=mesh['group'=8,'tensor'=8,'seq'=4] {'tensor'}, dimensions={0}, use_global_device_ids=true | all-gather | bytes 737280 | tf_op jit(solution)/shard_map/all_gather | solution.py:43
  33.1 0.2 convert_reduce_fusion
  33.3 0.3 fusion.22
  33.6 1.0 fusion.24
  34.6 2.0 convolution_convert_fusion.2
  36.6 0.0 all-gather.4.cloned.1.call-update
  36.6 0.0 all-gather.6.cloned.1.call-start
  36.7 0.0 copy-done.9
  36.7 1.0 convolution_convert_fusion.1
  37.7 0.0 all-gather.6.cloned.1.call-update
  37.7 0.0 all-reduce.2.cloned.1.call-start
  37.8 0.1 add_select_fusion.2
  37.9 0.4 convolution_convert_fusion.3
  38.3 1.2 broadcast_compare_fusion
  39.5 62.9 %all-gather.4.cloned.1.call-done = bf16[8192,160]{0,1:T(8,128)(2,1)} async-done(((bf16[256,160]{0,1:T(8,128)(2,1)}), bf16[8192,160]{0,1:T(8,128)(2,1)}) %all-gather.4.cloned.1.call-update) | async-done | bytes 2621456 | tf_op jit(solution)/shard_map/all_gather | solution.py:76
  102.4 5.6 %select_reduce_fusion = (f32[2,256]{1,0:T(2,128)S(1)}, f32[2,256,8192]{2,1,0:T(8,128)S(1)}) fusion(pred[256,8192]{1,0:T(8,128)(4,1)S(1)} %broadcast_compare_fusion, bf16[256,2,80]{0,2,1:T(8,128)(2,1)S(1)} %bitcast.128, bf16[8192,2,80]{0,2,1:T(8,128)(2,1)} %bitcast.126), kind=kOutput, calls=%fused_computation.2 | convolution fusion | flops 683671040 | bytes 21579776 | tf_op jit(solution)/shard_map/rhd,khd->hrk/dot_general | solution.py:84
  108.0 5.7 %copy-done.1 = f32[2,256,8192]{2,1,0:T(8,128)} copy-done((f32[2,256,8192]{2,1,0:T(8,128)}, f32[2,256,8192]{2,1,0:T(8,128)S(1)}, u32[]{:S(2)}) %copy-start.1) | copy-done | bytes 16777240
  113.7 4.8 %fusion.2 = f32[2,256]{1,0:T(2,128)S(1)} fusion(f32[2,256,8192]{2,1,0:T(8,128)S(1)} %get-tuple-element.6, f32[2,256]{1,0:T(2,128)S(1)} %broadcast_maximum_fusion, pred[256,8192]{1,0:T(8,128)(4,1)S(1)} %broadcast_compare_fusion), kind=kLoop, calls=%fused_computation.5 | loop fusion | flops 16776704 | bytes 18878464 | tf_op jit(solution)/shard_map/reduce_sum | solution.py:90
  118.5 41.9 %all-gather.6.cloned.1.call-done = bf16[8192,160]{0,1:T(8,128)(2,1)} async-done(((bf16[256,160]{0,1:T(8,128)(2,1)}), bf16[8192,160]{0,1:T(8,128)(2,1)}) %all-gather.6.cloned.1.call-update) | async-done | bytes 2621456 | tf_op jit(solution)/shard_map/all_gather | solution.py:77
  160.4 8.5 %fusion.35 = bf16[256,2,80]{0,2,1:T(8,128)(2,1)S(1)} fusion(bf16[8192,2,80]{0,2,1:T(8,128)(2,1)} %bitcast.127, f32[2,256,8192]{2,1,0:T(8,128)} %copy-done.1, f32[2,256]{1,0:T(2,128)S(1)} %broadcast_maximum_fusion, pred[256,8192]{1,0:T(8,128)(4,1)S(1)} %broadcast_compare_fusion, f32[256,2]{0,1:T(2,128)S(1)} %bitcast.123), kind=kOutput, calls=%fused_computation.42 | convolution fusion | flops 687947776 | bytes 21581824 | tf_op jit(solution)/shard_map/hrk,khd->hrd/dot_general | solution.py:91
  168.9 0.0 copy-start.6
  168.9 0.0 copy-start.2
  168.9 0.0 copy-start.10
  169.0 1.2 convolution_convert_fusion
  170.2 0.0 all-reduce.2.cloned.1.call-update
  170.2 0.2 all-gather.8.cloned.1.call-start
  170.4 74.0 %all-reduce.2.cloned.1.call-done = bf16[256,1280]{1,0:T(8,128)(2,1)} async-done(((bf16[256,1280]{1,0:T(8,128)(2,1)}), bf16[256,1280]{1,0:T(8,128)(2,1)}) %all-reduce.2.cloned.1.call-update) | async-done | bytes 655376 | tf_op jit(solution)/shard_map/psum | solution.py:101
  244.4 1.5 fusion.44
  246.0 0.1 multiply_convert_fusion
  246.1 0.7 pad_maximum_fusion
  246.8 0.0 all-gather.8.cloned.1.call-update
  246.8 0.5 fusion.12
  247.3 0.0 copy-start.7
  247.3 0.0 copy-start.4
  247.4 0.0 copy-start.5
  247.4 5.4 %fusion.100 = (f32[128,512]{1,0:T(8,128)S(1)}, f32[128,512]{1,0:T(8,128)}) fusion(bf16[8192,512]{1,0:T(8,128)(2,1)} %param.20, bf16[128,8192]{1,0:T(8,128)(2,1)S(1)} %copy-done.2, f32[8192]{0:T(1024)S(1)} %copy-done.10, f32[128]{0:T(128)S(1)} %add_rsqrt_fusion.3), kind=kOutput, calls=%fused_computation.160 | convolution fusion | flops 1078001664 | bytes 11043328 | tf_op jit(solution)/shard_map/dot_general | solution.py:121
  252.8 0.1 mul.214
  252.9 0.2 reduce_sum.70
  253.1 0.1 fusion.73
  253.2 0.0 copy-done.4
  253.2 0.0 copy-done.5
  253.2 2.8 compare_and_fusion
  256.0 58.9 %all-gather.8.cloned.1.call-done = bf16[8192,256]{0,1:T(8,128)(2,1)} async-done(((bf16[256,256]{0,1:T(8,128)(2,1)}), bf16[8192,256]{0,1:T(8,128)(2,1)}) %all-gather.8.cloned.1.call-update) | async-done | bytes 4194320 | tf_op jit(solution)/shard_map/all_gather | solution.py:116
  314.9 0.2 mul.215
  315.1 10.6 %fusion = (f32[4,128]{1,0:T(4,128)S(1)}, f32[8192,128,4]{1,0,2:T(8,128)}) fusion(pred[128,8192]{0,1:T(8,128)(4,1)S(1)} %compare_and_fusion, bf16[8192,1,2,128]{0,3,2,1:T(8,128)(2,1)} %bitcast.124, f32[128,512]{1,0:T(8,128)} %get-tuple-element.8, f32[16,8,4,128]{3,2,1,0:T(4,128)S(1)} %bitcast.120, f32[512]{0:T(512)S(1)} %broadcast_bitcast_fusion), kind=kOutput, calls=%fused_computation.3 | convolution fusion | flops 1082392064 | bytes 20451328 | tf_op jit(solution)/shard_map/rgqd,kgd->gqrk/dot_general | solution.py:134
  325.7 0.0 copy-done.8
  325.7 7.4 %fusion.41 = bf16[128,1,4,128]{0,3,2,1:T(8,128)(2,1)S(1)} fusion(f32[8192,128,4]{1,0,2:T(8,128)} %get-tuple-element.10, pred[128,8192]{0,1:T(8,128)(4,1)S(1)} %compare_and_fusion, bf16[8192,1,2,128]{0,3,2,1:T(8,128)(2,1)S(1)} %bitcast.125, f32[128,4]{0,1:T(4,128)S(1)} %bitcast.129), kind=kOutput, calls=%fused_computation.44 | convolution fusion | flops 1082261504 | bytes 20056064 | tf_op jit(solution)/shard_map/gqrk,kgd->rgqd/dot_general | solution.py:139
  333.1 0.8 copy.31
  (22 shorter events, 0.2 us)
Async XLA Ops:
  6.5 237.9 %copy-start = (bf16[1280,256]{1,0:T(8,128)(2,1)S(1)}, bf16[1280,256]{1,0:T(8,128)(2,1)}, u32[]{:S(2)}) copy-start(bf16[1280,256]{1,0:T(8,128)(2,1)} %param.16) | copy-start | bytes 1966084
  6.5 30.2 %copy-start.9 = (bf16[3,1280,160]{1,2,0:T(8,128)(2,1)S(1)}, bf16[3,1280,160]{1,2,0:T(8,128)(2,1)}, u32[]{:S(2)}) copy-start(bf16[3,1280,160]{1,2,0:T(8,128)(2,1)} %param.14) | copy-start | bytes 3686404
  6.5 95.9 %all-gather.4.cloned.1.call-start = ((), (), s32[]{:S(2)}) async-start(), calls=%async_computation | async-start | bytes 2703360 | tf_op jit(solution)/shard_map/all_gather | solution.py:76
  36.6 123.8 %all-gather.6.cloned.1.call-start = ((), (), s32[]{:S(2)}) async-start(), calls=%async_computation.1 | async-start | bytes 2703360 | tf_op jit(solution)/shard_map/all_gather | solution.py:77
  37.7 206.7 %all-reduce.2.cloned.1.call-start = ((), (), s32[]{:S(2)}) async-start(), calls=%async_computation.2 | async-start | bytes 1310720 | tf_op jit(solution)/shard_map/psum | solution.py:101
  108.0 5.7 %copy-start.1 = (f32[2,256,8192]{2,1,0:T(8,128)}, f32[2,256,8192]{2,1,0:T(8,128)S(1)}, u32[]{:S(2)}) copy-start(f32[2,256,8192]{2,1,0:T(8,128)S(1)} %get-tuple-element.6) | copy-start | bytes 50331652
  160.4 8.6 %copy-start.3 = (bf16[160,1280]{1,0:T(8,128)(2,1)S(1)}, bf16[160,1280]{1,0:T(8,128)(2,1)}, u32[]{:S(2)}) copy-start(bf16[160,1280]{1,0:T(8,128)(2,1)} %param.15) | copy-start | bytes 1228804
  168.9 77.1 %copy-start.6 = (f32[128]{0:T(128)S(1)}, f32[128]{0:T(128)}, u32[]{:S(2)}) copy-start(f32[128]{0:T(128)} %param.17) | copy-start | bytes 1540
  168.9 77.9 %copy-start.2 = (bf16[128,8192]{1,0:T(8,128)(2,1)S(1)}, bf16[128,8192]{1,0:T(8,128)(2,1)}, u32[]{:S(2)}) copy-start(bf16[128,8192]{1,0:T(8,128)(2,1)} %param.18) | copy-start | bytes 6291460
  168.9 78.4 %copy-start.10 = (f32[8192]{0:T(1024)S(1)}, f32[8192]{0:T(1024)}, u32[]{:S(2)}) copy-start(f32[8192]{0:T(1024)} %param.19) | copy-start | bytes 98308
  170.2 144.7 %all-gather.8.cloned.1.call-start = ((), (), s32[]{:S(2)}) async-start(), calls=%async_computation.3 | async-start | bytes 4325376 | tf_op jit(solution)/shard_map/all_gather | solution.py:116
  247.3 5.8 %copy-start.7 = (f32[128]{0:T(128)S(1)}, f32[128]{0:T(128)}, u32[]{:S(2)}) copy-start(f32[128]{0:T(128)} %param.21) | copy-start | bytes 1540
  247.3 5.8 %copy-start.4 = (s32[128]{0:T(128)S(1)}, s32[128]{0:T(128)}, u32[]{:S(2)}) copy-start(s32[128]{0:T(128)} %param.23) | copy-start | bytes 1540
  247.4 5.8 %copy-start.5 = (s32[128]{0:T(128)S(1)}, s32[128]{0:T(128)}, u32[]{:S(2)}) copy-start(s32[128]{0:T(128)} %param.22) | copy-start | bytes 1540
  315.1 10.6 %copy-start.8 = (bf16[8192,256]{0,1:T(8,128)(2,1)S(1)}, bf16[8192,256]{0,1:T(8,128)(2,1)}, u32[]{:S(2)}) copy-start(bf16[8192,256]{0,1:T(8,128)(2,1)} %all-gather.8.cloned.1.call-done) | copy-start | bytes 12582916
Sparse Core Ops, SparseCore 0:
  36.8 65.6 all-gather.3
  104.9 55.4 all-gather.5
  170.3 74.0 all-reduce.1
  246.9 67.8 all-gather.7
where the time goes:
time: 341 us; the launch traced here: 340 us
  waiting for transfers between devices  238 us (70%)
  matrix products  43.6 us (13%)
  blocking collectives  26.6 us (8%)
  between operations  13.4 us (4%)
  other arithmetic  11.9 us (3%)
  local copies, waits for them, and re-layouts  6.82 us (2%)
    psum x1, waiting for transfers between devices, on_device(): lax.psum(jnp.dot(attended, enc_out, preferred_element_type=jnp.float32).a...  74 us
    all_gather x1, waiting for transfers between devices, on_device(): key_shard = lax.all_gather(key_part, ('group', 'seq'), axis=0, tiled=True)  62.9 us
    all_gather x1, waiting for transfers between devices, on_device(): every_slab = lax.all_gather(kv_slab, ('group', 'seq'), axis=0, tiled=True)  58.9 us
    all_gather x1, waiting for transfers between devices, on_device(): lax.all_gather(value_part, ('group', 'seq'), axis=0, tiled=True)  41.9 us
    all_gather x1, blocking collectives, on_device(): gathered = lax.all_gather(patches, 'tensor', axis=0, tiled=True)  26.6 us
    dot_general x1, matrix products, on_device(): jnp.einsum('rgqd,kgd->gqrk', queries, slab_view[:, :, 0], preferred_eleme...  10.6 us
    dot_general x1, matrix products, on_device(): jnp.einsum('hrk,khd->hrd', weights.astype(jnp.bfloat16), value_heads, pre...  8.5 us
    dot_general x1, matrix products, on_device(): jnp.einsum('gqrk,kgd->rgqd', weights.astype(jnp.bfloat16), slab_view[:, :...  7.39 us
  transfers between devices with their start and end apart: 4, of which 4 were waited for; matrix products, arithmetic and copies ran while one was open for 7% of the time, Pallas kernels for 0%

commit v1 on v0

--- a/solution.py
+++ b/solution.py
@@ -98,9 +98,12 @@
     final_max, final_sum, final_mix = folded
     attended = (final_mix / final_sum[..., None]).astype(jnp.bfloat16)
     attended = attended.transpose(1, 0, 2).reshape(row_count, local_width)
-    total_out = lax.psum(
-        jnp.dot(attended, enc_out, preferred_element_type=jnp.float32).astype(jnp.bfloat16),
-        "tensor",
+    total_out = jnp.sum(
+        jax.lax.all_gather(
+            jnp.dot(attended, enc_out, preferred_element_type=jnp.float32).astype(jnp.bfloat16),
+            "tensor",
+        ),
+        axis=0,
     ).astype(jnp.float32)
     encoded = (gathered.astype(jnp.float32) + total_out).astype(jnp.bfloat16)
     kv_local = cross_kv.shape[1] // (2 * HD)

time: 341 us -> 375 us (1.100)
  waiting for transfers between devices: 238 us -> 269 us
  other arithmetic: 11.9 us -> 17.1 us
    all_gather x0 -> x1, waiting for transfers between devices: none -> 109 us  [on_device(): jax.lax.all_gather(jnp.dot(attended, enc_out, preferred_element_type=jnp....]
    psum x1 -> x0, waiting for transfers between devices: 74 us -> none  [on_device(): lax.psum(jnp.dot(attended, enc_out, preferred_element_type=jnp.float32).a...]
    all_gather x1, waiting for transfers between devices: 58.9 us -> 54.5 us  [on_device(): every_slab = lax.all_gather(kv_slab, ('group', 'seq'), axis=0, tiled=True)]
  transfers between devices with their start and end apart: 4 -> 4, of which waited for: 4 -> 4; matrix products, arithmetic and copies ran while one was open for 7% -> 6% of each run, Pallas kernels for 0% -> 0%
where the time goes in v1:
time: 375 us; the launch traced here: 374 us
  waiting for transfers between devices  269 us (72%)
  matrix products  41.5 us (11%)
  blocking collectives  26.6 us (7%)
  other arithmetic  17.1 us (5%)
  between operations  13.4 us (4%)
  local copies, waits for them, and re-layouts  6.81 us (2%)
    all_gather x1, waiting for transfers between devices, on_device(): jax.lax.all_gather(jnp.dot(attended, enc_out, preferred_element_type=jnp....  109 us
    all_gather x1, waiting for transfers between devices, on_device(): key_shard = lax.all_gather(key_part, ('group', 'seq'), axis=0, tiled=True)  62.9 us
    all_gather x1, waiting for transfers between devices, on_device(): every_slab = lax.all_gather(kv_slab, ('group', 'seq'), axis=0, tiled=True)  54.5 us
    all_gather x1, waiting for transfers between devices, on_device(): lax.all_gather(value_part, ('group', 'seq'), axis=0, tiled=True)  41.9 us
    all_gather x1, blocking collectives, on_device(): gathered = lax.all_gather(patches, 'tensor', axis=0, tiled=True)  26.6 us
    dot_general x1, matrix products, on_device(): jnp.einsum('rgqd,kgd->gqrk', queries, slab_view[:, :, 0], preferred_eleme...  9.56 us
    dot_general x1, matrix products, on_device(): jnp.einsum('hrk,khd->hrd', weights.astype(jnp.bfloat16), value_heads, pre...  8.5 us
  transfers between devices with their start and end apart: 4, of which 4 were waited for; matrix products, arithmetic and copies ran while one was open for 6% of the time, Pallas kernels for 0%

profile of v1, /device:TPU:1, one launch (start us, length us, event | category | flops | bytes accessed | tf_op | source)
XLA Modules:
  0.0 374.4 jit_solution(8979524236819842896)
XLA Ops:
  6.5 26.6 %all_gather.18 = bf16[256,1280]{1,0:T(8,128)(2,1)S(1)} all-gather(bf16[32,1280]{1,0:T(8,128)(2,1)} %param.12), channel_id=1, replica_groups=mesh['group'=8,'tensor'=8,'seq'=4] {'tensor'}, dimensions={0}, use_global_device_ids=true | all-gather | bytes 737280 | tf_op jit(solution)/shard_map/all_gather | solution.py:43
  33.1 0.2 convert_reduce_fusion
  33.3 0.3 fusion.22
  33.6 1.0 fusion.24
  34.6 2.0 convolution_convert_fusion.2
  36.6 0.0 all-gather.6.cloned.1.call-update
  36.6 0.0 all-gather.8.cloned.1.call-start
  36.7 0.0 copy-done.9
  36.7 1.0 convolution_convert_fusion.1
  37.7 0.0 all-gather.8.cloned.1.call-update
  37.7 0.0 all-gather.12.cloned.1.call-start
  37.8 0.1 add_select_fusion.2
  37.9 0.4 convolution_convert_fusion.3
  38.3 1.2 broadcast_compare_fusion
  39.5 62.9 %all-gather.6.cloned.1.call-done = bf16[8192,160]{0,1:T(8,128)(2,1)} async-done(((bf16[256,160]{0,1:T(8,128)(2,1)}), bf16[8192,160]{0,1:T(8,128)(2,1)}) %all-gather.6.cloned.1.call-update) | async-done | bytes 2621456 | tf_op jit(solution)/shard_map/all_gather | solution.py:76
  102.4 5.6 %select_reduce_fusion = (f32[2,256]{1,0:T(2,128)S(1)}, f32[2,256,8192]{2,1,0:T(8,128)S(1)}) fusion(pred[256,8192]{1,0:T(8,128)(4,1)S(1)} %broadcast_compare_fusion, bf16[256,2,80]{0,2,1:T(8,128)(2,1)S(1)} %bitcast.130, bf16[8192,2,80]{0,2,1:T(8,128)(2,1)} %bitcast.128), kind=kOutput, calls=%fused_computation.2 | convolution fusion | flops 683671040 | bytes 21579776 | tf_op jit(solution)/shard_map/rhd,khd->hrk/dot_general | solution.py:84
  108.0 5.7 %copy-done.2 = f32[2,256,8192]{2,1,0:T(8,128)} copy-done((f32[2,256,8192]{2,1,0:T(8,128)}, f32[2,256,8192]{2,1,0:T(8,128)S(1)}, u32[]{:S(2)}) %copy-start.2) | copy-done | bytes 16777240
  113.7 4.8 %fusion.2 = f32[2,256]{1,0:T(2,128)S(1)} fusion(f32[2,256,8192]{2,1,0:T(8,128)S(1)} %get-tuple-element.6, f32[2,256]{1,0:T(2,128)S(1)} %broadcast_maximum_fusion, pred[256,8192]{1,0:T(8,128)(4,1)S(1)} %broadcast_compare_fusion), kind=kLoop, calls=%fused_computation.5 | loop fusion | flops 16776704 | bytes 18878464 | tf_op jit(solution)/shard_map/reduce_sum | solution.py:90
  118.5 41.9 %all-gather.8.cloned.1.call-done = bf16[8192,160]{0,1:T(8,128)(2,1)} async-done(((bf16[256,160]{0,1:T(8,128)(2,1)}), bf16[8192,160]{0,1:T(8,128)(2,1)}) %all-gather.8.cloned.1.call-update) | async-done | bytes 2621456 | tf_op jit(solution)/shard_map/all_gather | solution.py:77
  160.4 8.5 %fusion.35 = bf16[256,2,80]{0,2,1:T(8,128)(2,1)S(1)} fusion(bf16[8192,2,80]{0,2,1:T(8,128)(2,1)} %bitcast.129, f32[2,256,8192]{2,1,0:T(8,128)} %copy-done.2, f32[2,256]{1,0:T(2,128)S(1)} %broadcast_maximum_fusion, pred[256,8192]{1,0:T(8,128)(4,1)S(1)} %broadcast_compare_fusion, f32[256,2]{0,1:T(2,128)S(1)} %bitcast.125), kind=kOutput, calls=%fused_computation.42 | convolution fusion | flops 687947776 | bytes 21581824 | tf_op jit(solution)/shard_map/hrk,khd->hrd/dot_general | solution.py:91
  168.9 0.0 copy-done.3
  168.9 1.2 convolution_convert_fusion
  170.2 0.0 all-gather.12.cloned.1.call-update
  170.2 0.2 all-gather.10.cloned.1.call-start
  170.4 109.4 %all-gather.12.cloned.1.call-done = bf16[2048,1280]{1,0:T(8,128)(2,1)} async-done(((bf16[256,1280]{1,0:T(8,128)(2,1)}), bf16[2048,1280]{1,0:T(8,128)(2,1)}) %all-gather.12.cloned.1.call-update) | async-done | bytes 5242896 | tf_op jit(solution)/shard_map/all_gather | solution.py:102
  279.8 3.6 reduce_sum.80
  283.4 0.0 copy-done
  283.4 0.5 fusion.44
  283.9 0.0 copy-done.6
  283.9 0.1 multiply_convert_fusion
  284.0 0.7 pad_maximum_fusion
  284.7 0.0 all-gather.10.cloned.1.call-update
  284.7 2.1 fusion.12
  286.8 0.0 copy-start.7
  286.8 0.0 copy-start.4
  286.8 0.0 copy-start.5
  286.8 5.3 %fusion.100 = (f32[128,512]{1,0:T(8,128)S(1)}, f32[128,512]{1,0:T(8,128)S(1)}) fusion(bf16[8192,512]{1,0:T(8,128)(2,1)} %param.20, bf16[128,8192]{1,0:T(8,128)(2,1)} %param.18, f32[8192]{0:T(1024)S(1)} %copy-done.10, f32[128]{0:T(128)S(1)} %add_rsqrt_fusion.3), kind=kOutput, calls=%fused_computation.160 | convolution fusion | flops 1078001664 | bytes 11043328 | tf_op jit(solution)/shard_map/dot_general | solution.py:124
  292.2 0.1 mul.214
  292.3 0.2 reduce_sum.83
  292.5 0.1 fusion.73
  292.6 2.8 compare_and_fusion
  295.4 54.5 %all-gather.10.cloned.1.call-done = bf16[8192,256]{0,1:T(8,128)(2,1)} async-done(((bf16[256,256]{0,1:T(8,128)(2,1)}), bf16[8192,256]{0,1:T(8,128)(2,1)}) %all-gather.10.cloned.1.call-update) | async-done | bytes 4194320 | tf_op jit(solution)/shard_map/all_gather | solution.py:119
  349.9 0.2 mul.215
  350.1 0.0 copy-start.8
  350.1 9.6 %fusion = (f32[4,128]{1,0:T(4,128)S(1)}, f32[8192,128,4]{1,0,2:T(8,128)}) fusion(pred[128,8192]{0,1:T(8,128)(4,1)S(1)} %compare_and_fusion, bf16[8192,1,2,128]{0,3,2,1:T(8,128)(2,1)} %bitcast.126, f32[128,512]{1,0:T(8,128)S(1)} %get-tuple-element.8, f32[16,8,4,128]{3,2,1,0:T(4,128)S(1)} %bitcast.122, f32[512]{0:T(512)S(1)} %broadcast_bitcast_fusion), kind=kOutput, calls=%fused_computation.3 | convolution fusion | flops 1082392064 | bytes 20451328 | tf_op jit(solution)/shard_map/rgqd,kgd->gqrk/dot_general | solution.py:137
  359.7 7.5 %fusion.41 = bf16[128,1,4,128]{0,3,2,1:T(8,128)(2,1)S(1)} fusion(f32[8192,128,4]{1,0,2:T(8,128)} %get-tuple-element.10, pred[128,8192]{0,1:T(8,128)(4,1)S(1)} %compare_and_fusion, bf16[8192,1,2,128]{0,3,2,1:T(8,128)(2,1)S(1)} %bitcast.127, f32[128,4]{0,1:T(4,128)S(1)} %bitcast.131), kind=kOutput, calls=%fused_computation.44 | convolution fusion | flops 1082261504 | bytes 20056064 | tf_op jit(solution)/shard_map/gqrk,kgd->rgqd/dot_general | solution.py:142
  367.1 0.8 copy.31
  367.9 0.0 copy-done.1
  (23 shorter events, 0.2 us)
Async XLA Ops:
  6.5 276.8 %copy-start = (bf16[1280,256]{1,0:T(8,128)(2,1)S(1)}, bf16[1280,256]{1,0:T(8,128)(2,1)}, u32[]{:S(2)}) copy-start(bf16[1280,256]{1,0:T(8,128)(2,1)} %param.16) | copy-start | bytes 1966084
  6.5 30.2 %copy-start.9 = (bf16[3,1280,160]{1,2,0:T(8,128)(2,1)S(1)}, bf16[3,1280,160]{1,2,0:T(8,128)(2,1)}, u32[]{:S(2)}) copy-start(bf16[3,1280,160]{1,2,0:T(8,128)(2,1)} %param.14) | copy-start | bytes 3686404
  6.5 95.9 %all-gather.6.cloned.1.call-start = ((), (), s32[]{:S(2)}) async-start(), calls=%async_computation | async-start | bytes 2703360 | tf_op jit(solution)/shard_map/all_gather | solution.py:76
  36.6 123.8 %all-gather.8.cloned.1.call-start = ((), (), s32[]{:S(2)}) async-start(), calls=%async_computation.1 | async-start | bytes 2703360 | tf_op jit(solution)/shard_map/all_gather | solution.py:77
  37.7 242.1 %all-gather.12.cloned.1.call-start = ((), (), s32[]{:S(2)}) async-start(), calls=%async_computation.3 | async-start | bytes 5898240 | tf_op jit(solution)/shard_map/all_gather | solution.py:102
  108.0 5.7 %copy-start.2 = (f32[2,256,8192]{2,1,0:T(8,128)}, f32[2,256,8192]{2,1,0:T(8,128)S(1)}, u32[]{:S(2)}) copy-start(f32[2,256,8192]{2,1,0:T(8,128)S(1)} %get-tuple-element.6) | copy-start | bytes 50331652
  160.4 8.5 %copy-start.3 = (bf16[160,1280]{1,0:T(8,128)(2,1)S(1)}, bf16[160,1280]{1,0:T(8,128)(2,1)}, u32[]{:S(2)}) copy-start(bf16[160,1280]{1,0:T(8,128)(2,1)} %param.15) | copy-start | bytes 1228804
  170.2 179.7 %all-gather.10.cloned.1.call-start = ((), (), s32[]{:S(2)}) async-start(), calls=%async_computation.2 | async-start | bytes 4325376 | tf_op jit(solution)/shard_map/all_gather | solution.py:119
  279.8 4.1 %copy-start.6 = (f32[128]{0:T(128)S(1)}, f32[128]{0:T(128)}, u32[]{:S(2)}) copy-start(f32[128]{0:T(128)} %param.17) | copy-start | bytes 1540
  279.8 7.0 %copy-start.10 = (f32[8192]{0:T(1024)S(1)}, f32[8192]{0:T(1024)}, u32[]{:S(2)}) copy-start(f32[8192]{0:T(1024)} %param.19) | copy-start | bytes 98308
  286.8 5.8 %copy-start.7 = (f32[128]{0:T(128)S(1)}, f32[128]{0:T(128)}, u32[]{:S(2)}) copy-start(f32[128]{0:T(128)} %param.21) | copy-start | bytes 1540
  286.8 5.8 %copy-start.4 = (s32[128]{0:T(128)S(1)}, s32[128]{0:T(128)}, u32[]{:S(2)}) copy-start(s32[128]{0:T(128)} %param.23) | copy-start | bytes 1540
  286.8 5.8 %copy-start.5 = (s32[128]{0:T(128)S(1)}, s32[128]{0:T(128)}, u32[]{:S(2)}) copy-start(s32[128]{0:T(128)} %param.22) | copy-start | bytes 1540
  350.1 9.6 %copy-start.8 = (bf16[8192,256]{0,1:T(8,128)(2,1)S(1)}, bf16[8192,256]{0,1:T(8,128)(2,1)}, u32[]{:S(2)}) copy-start(bf16[8192,256]{0,1:T(8,128)(2,1)} %all-gather.10.cloned.1.call-done) | copy-start | bytes 12582916
  359.7 8.2 %copy-start.1 = (bf16[1280,256]{1,0:T(8,128)(2,1)S(1)}, bf16[1280,256]{1,0:T(8,128)(2,1)}, u32[]{:S(2)}) copy-start(bf16[1280,256]{1,0:T(8,128)(2,1)} %param.16) | copy-start | bytes 1966084
Sparse Core Ops, SparseCore 0:
  36.8 65.6 all-gather.5
  104.9 55.4 all-gather.7
  170.3 109.4 all-gather.11
  284.8 65.0 all-gather.9
